TPU v7x, 256 devices: a whole 4x4x8 slice. The times are simulated.
256 devices in a mesh: dp: 4 (over x), mp: 64 (over z, y, core).
Axes of the slice: x: 4, y: 4, z: 8, core: 2. Of those that a mesh axis runs over, the one named last changes fastest.
Arguments:
- residual: bfloat16 [1024, 4096], P(('dp', 'mp')), may hold values from -6 to 6
- ffn_gain: float32 [4096], replicated, may hold values from 0.5 to 1.5
- gate_weight: bfloat16 [4096, 8192], P(None, 'mp'), may hold values from -0.09375 to 0.09375
- up_weight: bfloat16 [4096, 8192], P(None, 'mp'), may hold values from -0.09375 to 0.09375
- down_weight: bfloat16 [8192, 4096], P('mp'), may hold values from -0.0625 to 0.0625
- final_gain: float32 [4096], replicated, may hold values from 0.5 to 1.5
- head_weight: bfloat16 [4096, 65536], P(None, 'mp')
- passage_ids: int32 [4, 256], P('dp'), may hold values from 0 to 3, never falling along the last dimension, each value on 1 to 128 neighbouring positions
- valid_counts: int32 [4, 4], P('dp'), may hold values from 1 to 128
Outputs:
- term_weights: float32 [16, 65536], P('dp', 'mp')
- entropy: float32 [], replicated
- grad_hidden: float32 [1024, 4096], P(('dp', 'mp'))
Inputs may be any that keep to these rules, and one draw needn't show every extreme that they name: `passage_ids`: within each group the ids never fall and every passage of 0 to 3 has 1 to 128 rows.
All inputs are finite; a program needn't handle non-finite values.
Results may differ from a plain program's by a relative error of at most 0.0069.
The roundings to bfloat16 on the way count: a program that leaves them out, or rounds other values in their place, can miss the bound.
Values may be sent and summed in bfloat16 or wider, within the bound.
No kernel may reach another device: no remote copies, remote signals or barrier semaphores. Data moves between devices by JAX's collectives and lax.ppermute only.
A program may use at most 64 MiB of HBM per device.

v0:
```python
import jax
import jax.numpy as jnp
from jax import lax
from jax.sharding import PartitionSpec as P


def rms_scale(values):
    return lax.rsqrt(jnp.mean(values * values, axis=-1, keepdims=True) + 1e-05)


def pool_masks(ids, counts):
    slots = jnp.arange(counts.shape[0], dtype=jnp.int32)
    member = ids[:, None] == slots[None, :]
    starts = jnp.sum((ids[:, None] < slots[None, :]).astype(jnp.int32), axis=0)
    start_row = jnp.sum(jnp.where(member, starts[None, :], 0), axis=1)
    count_row = jnp.sum(jnp.where(member, counts[None, :], 0), axis=1)
    position = jnp.arange(ids.shape[0], dtype=jnp.int32) - start_row
    valid = (position < count_row).astype(jnp.float32)
    return (member.astype(jnp.float32), valid)


def sum_groups(local_mass):
    return 1.0 + lax.psum(local_mass, "dp")


def body(
    residual,
    ffn_gain,
    gate_weight,
    up_weight,
    down_weight,
    final_gain,
    head_weight,
    passage_ids,
    valid_counts,
):
    highest = lax.Precision.HIGHEST
    own_rows = residual.astype(jnp.float32)
    tok_rows = own_rows.shape[0]
    group_rows = tok_rows * lax.axis_size("mp")
    normed_in = (own_rows * rms_scale(own_rows) * ffn_gain).astype(jnp.bfloat16)
    gathered = lax.all_gather(normed_in, "mp", axis=0, tiled=True)
    offset = lax.axis_index("mp") * tok_rows
    placed = lax.dynamic_update_slice_in_dim(
        jnp.zeros((group_rows, own_rows.shape[1]), jnp.float32), own_rows, offset, 0
    )
    row_block = gathered
    gate_vals = jnp.dot(row_block, gate_weight, preferred_element_type=jnp.float32)
    up_vals = jnp.dot(row_block, up_weight, preferred_element_type=jnp.float32)
    activated = (jax.nn.silu(gate_vals) * up_vals).astype(jnp.bfloat16)
    hidden_all = lax.psum(
        jnp.dot(activated, down_weight, preferred_element_type=jnp.float32) + placed, "mp"
    )
    scale_all = rms_scale(hidden_all)
    normed_all = (hidden_all * scale_all * final_gain).astype(jnp.bfloat16)
    logits = jnp.dot(normed_all, head_weight, preferred_element_type=jnp.float32)
    hidden = lax.dynamic_slice_in_dim(hidden_all, offset, tok_rows, 0)
    scale = lax.dynamic_slice_in_dim(scale_all, offset, tok_rows, 0)
    member, valid = pool_masks(passage_ids[0], valid_counts[0])
    weights = jnp.log1p(jnp.maximum(logits, 0.0))
    powered = valid[:, None] * weights**4
    pooled_sum = lax.dot_general(member, powered, (((0,), (0,)), ((), ())), precision=highest)
    term_weights = (1.0 + pooled_sum) ** 0.25 - 1.0
    local_mass = jnp.sum(term_weights, axis=0)
    smooth = sum_groups(local_mass)
    total = lax.psum(jnp.sum(smooth), "mp")
    spread = lax.psum(jnp.sum(smooth * jnp.log(smooth)), "mp")
    entropy = jnp.log(total) - spread / total
    slope_mass = jnp.log(total) - jnp.log(smooth)
    factor = (1.0 + pooled_sum) ** (-0.75)
    row_factor = jnp.dot(member, factor, precision=highest)
    slope_logit = (
        valid[:, None]
        * weights**3
        * row_factor
        * slope_mass[None, :]
        / (1.0 + jnp.maximum(logits, 0.0))
    ).astype(jnp.bfloat16)
    row_block = slope_logit
    slope_normed = lax.psum_scatter(
        lax.dot_general(
            row_block, head_weight, (((1,), (1,)), ((), ())), preferred_element_type=jnp.float32
        ),
        "mp",
        scatter_dimension=0,
        tiled=True,
    )
    scaled_slope = slope_normed * final_gain
    grad_hidden = scale * scaled_slope - hidden * scale**3 * jnp.mean(
        scaled_slope * hidden, axis=-1, keepdims=True
    )
    return (term_weights, entropy, grad_hidden)


def solution(mesh):
    placed = (
        P(("dp", "mp"), None),
        P(),
        P(None, "mp"),
        P(None, "mp"),
        P("mp", None),
        P(),
        P(None, "mp"),
        P("dp", None),
        P("dp", None),
    )
    return jax.shard_map(
        body,
        mesh=mesh,
        in_specs=placed,
        out_specs=(P("dp", "mp"), P(), P(("dp", "mp"), None)),
        check_vma=False,
    )
```

profile of v0, /device:TPU:2, one launch (start us, length us, event | category | flops | bytes accessed | tf_op | source)
XLA Modules:
  0.0 654.6 jit_solution(14113057163606590066)
XLA Ops:
  7.2 0.0 copy-start
  7.2 0.0 all-gather.3.cloned.1.call-start
  7.2 1.0 fusion.19
  8.2 1.5 fusion.24
  9.7 0.0 all-gather.3.cloned.1.call-update
  9.7 0.0 all-reduce.5.cloned.1.call-start
  9.8 82.1 %all-gather.3.cloned.1.call-done = bf16[64,4,4096]{2,1,0:T(4,128)(2,1)} async-done(((bf16[1,4,4096]{2,1,0:T(4,128)(2,1)}), bf16[64,4,4096]{2,1,0:T(4,128)(2,1)}) %all-gather.3.cloned.1.call-update) | async-done | bytes 2097168 | tf_op jit(solution)/shard_map/all_gather | solution.py:42
  91.9 2.5 reshape.57
  94.5 1.9 fusion.34
  96.4 0.0 copy-done
  96.4 0.0 copy-start.2
  96.4 4.5 fusion.8
  100.9 0.0 copy-done.2
  100.9 0.0 copy-start.4
  100.9 0.0 copy-start.5
  100.9 1.6 fusion.22
  102.5 0.0 copy-start.3
  102.5 0.0 all-reduce.5.cloned.1.call-update
  102.5 0.0 all-reduce.7.cloned.1.call-start
  102.6 0.0 copy-done.4
  102.6 0.1 convert_reduce_fusion
  102.7 0.0 copy-done.5
  102.7 0.1 select_reduce_fusion.1
  102.8 193.2 %all-reduce.5.cloned.1.call-done = f32[256,4096]{1,0:T(8,128)} async-done(((f32[256,4096]{1,0:T(8,128)}), f32[256,4096]{1,0:T(8,128)}) %all-reduce.5.cloned.1.call-update) | async-done | bytes 4194320 | tf_op jit(solution)/shard_map/psum | solution.py:51
  296.1 0.0 copy-start.1
  296.1 2.7 multiply_reduce_fusion
  298.8 0.0 copy-done.3
  298.8 0.7 copy-done.1
  299.5 5.8 fusion.5
  305.3 1.5 fusion.33
  306.8 8.6 %psum.29 = f32[1024]{0:T(1024)S(1)} all-reduce(f32[1024]{0:T(1024)S(1)} %get-tuple-element.11), channel_id=1, replica_groups=mesh['dp'=4,'mp'=64] {'dp'}, use_global_device_ids=true, to_apply=%region_7.8 | all-reduce | flops 1024 | bytes 8192 | tf_op jit(solution)/shard_map/psum | solution.py:23
  315.3 0.6 fusion.27
  315.9 126.2 %all-reduce.1 = (f32[]{:T(128)}, f32[]{:T(128)}) all-reduce(f32[]{:T(128)} %get-tuple-element.4, f32[]{:T(128)} %get-tuple-element.3), channel_id=1, replica_groups=mesh['dp'=4,'mp'=64] {'mp'}, use_global_device_ids=true, to_apply=%region_9.10 | all-reduce | flops 2 | bytes 16 | tf_op jit(solution)/shard_map/psum | solution.py:66
  442.8 1.1 fusion.6
  443.9 7.7 %fusion.35 = f32[256,4096]{1,0:T(8,128)} fusion(bf16[256,1024]{1,0:T(8,128)(2,1)S(1)} %fusion.6, bf16[4096,1024]{1,0:T(8,128)(2,1)} %param.15), kind=kOutput, calls=%fused_computation.61 | convolution fusion | flops 2147483648 | bytes 13107200 | tf_op jit(solution)/shard_map/dot_general | solution.py:81
  451.7 0.0 copy-start.6
  451.7 0.0 all-reduce.7.cloned.1.call-update
  451.7 0.6 copy-done.6
  452.4 0.6 dynamic-slice.5
  454.9 0.1 fusion.30
  455.0 189.1 %all-reduce.7.cloned.1.call-done = f32[256,4096]{1,0:T(8,128)} async-done(((f32[256,4096]{1,0:T(8,128)}), f32[256,4096]{1,0:T(8,128)}) %all-reduce.7.cloned.1.call-update) | async-done | bytes 4194320
  644.1 1.1 multiply_reduce_fusion.1
  645.2 1.7 multiply_subtract_fusion
  (5 shorter events, 0.0 us)
Async XLA Ops:
  7.2 89.2 %copy-start = (bf16[128,4096]{1,0:T(8,128)(2,1)S(1)}, bf16[128,4096]{1,0:T(8,128)(2,1)}, u32[]{:S(2)}) copy-start(bf16[128,4096]{1,0:T(8,128)(2,1)} %param.13) | copy-start | bytes 3145732
  7.2 84.7 %all-gather.3.cloned.1.call-start = ((), (), s32[]{:S(2)}) async-start(), calls=%async_computation.1 | async-start | bytes 2129920 | tf_op jit(solution)/shard_map/all_gather | solution.py:42
  9.7 286.3 %all-reduce.5.cloned.1.call-start = ((), (), s32[]{:S(2)}) async-start(), calls=%async_computation | async-start | bytes 8388608 | tf_op jit(solution)/shard_map/psum | solution.py:51
  96.4 4.5 copy-start.2
  100.9 1.7 copy-start.4
  100.9 1.8 copy-start.5
  102.5 196.2 %copy-start.3 = (f32[4096]{0:T(1024)S(1)}, f32[4096]{0:T(1024)}, u32[]{:S(2)}) copy-start(f32[4096]{0:T(1024)} %param.14) | copy-start | bytes 49156
  102.5 541.5 %all-reduce.7.cloned.1.call-start = ((), (), s32[]{:S(2)}) async-start(), calls=%async_computation.2 | async-start | bytes 8388608
  296.1 3.4 copy-start.1
  451.7 0.7 copy-start.6
Sparse Core Ops, SparseCore 0:
  11.3 80.5 all-gather.2
  102.7 193.3 all-reduce.4
  451.8 192.2 all-reduce.6
where the time goes:
time: 655 us
  waiting for transfers between devices  465 us (71%)
  blocking collectives  135 us (21%)
  matrix products  22.5 us (3%)
  between operations  17.6 us (3%)
  other arithmetic  10.5 us (2%)
    psum x1, waiting for transfers between devices, body(): lax.psum(jnp.dot(activated, down_weight, preferred_element_type=jnp.float...  193 us
    unnamed x4, waiting for transfers between devices  189 us
    psum x1, blocking collectives, body(): total = lax.psum(jnp.sum(smooth), 'mp')  126 us
    all_gather x1, waiting for transfers between devices, body(): gathered = lax.all_gather(normed_in, 'mp', axis=0, tiled=True)  82.1 us
  transfers between devices with their start and end apart: 3, of which 3 were waited for; matrix products, arithmetic and copies ran while one was open for 0% of the time, Pallas kernels for 0%

commit v1 on v0

--- a/solution.py
+++ b/solution.py
@@ -39,7 +39,9 @@
     tok_rows = own_rows.shape[0]
     group_rows = tok_rows * lax.axis_size("mp")
     normed_in = (own_rows * rms_scale(own_rows) * ffn_gain).astype(jnp.bfloat16)
-    gathered = lax.all_gather(normed_in, "mp", axis=0, tiled=True)
+    gathered = jnp.concatenate(
+        lax.all_to_all(jnp.stack([normed_in] * lax.axis_size("mp")), "mp", 0, 0), axis=0
+    )
     offset = lax.axis_index("mp") * tok_rows
     placed = lax.dynamic_update_slice_in_dim(
         jnp.zeros((group_rows, own_rows.shape[1]), jnp.float32), own_rows, offset, 0

time: 655 us -> 637 us (0.973)
  waiting for transfers between devices: 465 us -> 432 us
  starting transfers between devices: 0.12 us -> 12.5 us
    all_gather x1 -> x0, waiting for transfers between devices: 82.1 us -> none  [body(): gathered = lax.all_gather(normed_in, 'mp', axis=0, tiled=True)]
    all_to_all x0 -> x1, waiting for transfers between devices: none -> 51.1 us  [body(): lax.all_to_all(jnp.stack([normed_in] * lax.axis_size('mp')), 'mp', 0, 0)]
    all_to_all x0 -> x1, starting transfers between devices: none -> 12.4 us  [body(): lax.all_to_all(jnp.stack([normed_in] * lax.axis_size('mp')), 'mp', 0, 0)]
    unnamed x4 -> x3, waiting for transfers between devices: 189 us -> 189 us
where the time goes in v1:
time: 637 us
  waiting for transfers between devices  432 us (68%)
  blocking collectives  135 us (21%)
  matrix products  22.5 us (4%)
  between operations  17.9 us (3%)
  starting transfers between devices  12.5 us (2%)
  other arithmetic  9.87 us (2%)
  local copies, waits for them, and re-layouts  6.86 us (1%)
    psum x1, waiting for transfers between devices, body(): lax.psum(jnp.dot(activated, down_weight, preferred_element_type=jnp.float...  192 us
    unnamed x3, waiting for transfers between devices  189 us
    psum x1, blocking collectives, body(): total = lax.psum(jnp.sum(smooth), 'mp')  126 us
    all_to_all x1, waiting for transfers between devices, body(): lax.all_to_all(jnp.stack([normed_in] * lax.axis_size('mp')), 'mp', 0, 0)  51.1 us
  transfers between devices with their start and end apart: 3, of which 3 were waited for; matrix products, arithmetic and copies ran while one was open for 0% of the time, Pallas kernels for 0%

profile of v1, /device:TPU:2, one launch (start us, length us, event | category | flops | bytes accessed | tf_op | source)
XLA Modules:
  0.0 636.9 jit_solution(12310213831496150170)
XLA Ops:
  7.2 0.0 copy-start
  7.2 1.0 fusion.19
  8.2 0.9 fusion.21
  9.0 2.3 stack.2
  11.3 12.4 %all-to-all-start = ((bf16[64,4,4096]{2,1,0:T(4,128)(2,1)}), bf16[64,4,4096]{2,1,0:T(4,128)(2,1)}, u32[]{:S(2)}, u32[]{:S(2)}) async-start(bf16[64,4,4096]{2,1,0:T(4,128)(2,1)} %stack.2), calls=%async_computation | async-start | bytes 4194304 | tf_op jit(solution)/shard_map/all_to_all | solution.py:43
  23.7 0.0 all-reduce.5.cloned.1.call-start
  23.8 51.1 %all-to-all-done = bf16[64,4,4096]{2,1,0:T(4,128)(2,1)} async-done(((bf16[64,4,4096]{2,1,0:T(4,128)(2,1)}), bf16[64,4,4096]{2,1,0:T(4,128)(2,1)}, u32[]{:S(2)}, u32[]{:S(2)}) %all-to-all-start) | async-done | bytes 2097184 | tf_op jit(solution)/shard_map/all_to_all | solution.py:43
  74.9 2.5 reshape.61
  77.4 1.9 fusion.33
  79.4 0.0 copy-done
  79.4 0.0 copy-start.2
  79.4 4.5 fusion.8
  83.9 0.0 copy-done.2
  83.9 0.0 copy-start.4
  83.9 0.0 copy-start.5
  83.9 1.6 fusion.22
  85.5 0.0 copy-start.3
  85.5 0.0 all-reduce.5.cloned.1.call-update
  85.5 0.0 all-reduce.7.cloned.1.call-start
  85.6 0.0 copy-done.4
  85.6 0.1 convert_reduce_fusion
  85.7 0.0 copy-done.5
  85.7 0.1 select_reduce_fusion.1
  85.8 192.3 %all-reduce.5.cloned.1.call-done = f32[256,4096]{1,0:T(8,128)} async-done(((f32[256,4096]{1,0:T(8,128)}), f32[256,4096]{1,0:T(8,128)}) %all-reduce.5.cloned.1.call-update) | async-done | bytes 4194320 | tf_op jit(solution)/shard_map/psum | solution.py:53
  278.1 0.0 copy-start.1
  278.1 2.7 multiply_reduce_fusion
  280.8 0.0 copy-done.3
  280.8 0.7 copy-done.1
  281.5 5.8 fusion.5
  287.3 1.5 fusion.32
  288.8 8.6 %psum.29 = f32[1024]{0:T(1024)S(1)} all-reduce(f32[1024]{0:T(1024)S(1)} %get-tuple-element.11), channel_id=1, replica_groups=mesh['dp'=4,'mp'=64] {'dp'}, use_global_device_ids=true, to_apply=%region_7.8 | all-reduce | flops 1024 | bytes 8192 | tf_op jit(solution)/shard_map/psum | solution.py:23
  297.3 0.6 fusion.26
  297.9 126.2 %all-reduce.1 = (f32[]{:T(128)}, f32[]{:T(128)}) all-reduce(f32[]{:T(128)} %get-tuple-element.4, f32[]{:T(128)} %get-tuple-element.3), channel_id=1, replica_groups=mesh['dp'=4,'mp'=64] {'mp'}, use_global_device_ids=true, to_apply=%region_9.10 | all-reduce | flops 2 | bytes 16 | tf_op jit(solution)/shard_map/psum | solution.py:68
  424.8 1.1 fusion.6
  426.0 7.7 %fusion.34 = f32[256,4096]{1,0:T(8,128)} fusion(bf16[256,1024]{1,0:T(8,128)(2,1)S(1)} %fusion.6, bf16[4096,1024]{1,0:T(8,128)(2,1)} %param.15), kind=kOutput, calls=%fused_computation.60 | convolution fusion | flops 2147483648 | bytes 13107200 | tf_op jit(solution)/shard_map/dot_general | solution.py:83
  433.7 0.0 copy-start.6
  433.7 0.0 all-reduce.7.cloned.1.call-update
  433.7 0.6 copy-done.6
  434.4 0.6 dynamic-slice.5
  436.9 0.1 fusion.29
  437.0 189.1 %all-reduce.7.cloned.1.call-done = f32[256,4096]{1,0:T(8,128)} async-done(((f32[256,4096]{1,0:T(8,128)}), f32[256,4096]{1,0:T(8,128)}) %all-reduce.7.cloned.1.call-update) | async-done | bytes 4194320
  626.1 1.1 multiply_reduce_fusion.1
  627.2 1.7 multiply_subtract_fusion
  (5 shorter events, 0.0 us)
Async XLA Ops:
  7.2 72.2 %copy-start = (bf16[128,4096]{1,0:T(8,128)(2,1)S(1)}, bf16[128,4096]{1,0:T(8,128)(2,1)}, u32[]{:S(2)}) copy-start(bf16[128,4096]{1,0:T(8,128)(2,1)} %param.13) | copy-start | bytes 3145732
  11.3 63.6 %all-to-all-start = ((bf16[64,4,4096]{2,1,0:T(4,128)(2,1)}), bf16[64,4,4096]{2,1,0:T(4,128)(2,1)}, u32[]{:S(2)}, u32[]{:S(2)}) async-start(bf16[64,4,4096]{2,1,0:T(4,128)(2,1)} %stack.2), calls=%async_computation | async-start | bytes 4194304 | tf_op jit(solution)/shard_map/all_to_all | solution.py:43
  23.7 254.4 %all-reduce.5.cloned.1.call-start = ((), (), s32[]{:S(2)}) async-start(), calls=%async_computation.1 | async-start | bytes 8388608 | tf_op jit(solution)/shard_map/psum | solution.py:53
  79.4 4.5 copy-start.2
  83.9 1.7 copy-start.4
  83.9 1.8 copy-start.5
  85.5 195.3 %copy-start.3 = (f32[4096]{0:T(1024)S(1)}, f32[4096]{0:T(1024)}, u32[]{:S(2)}) copy-start(f32[4096]{0:T(1024)} %param.14) | copy-start | bytes 49156
  85.5 540.6 %all-reduce.7.cloned.1.call-start = ((), (), s32[]{:S(2)}) async-start(), calls=%async_computation.2 | async-start | bytes 8388608
  278.1 3.4 copy-start.1
  433.7 0.7 copy-start.6
Sparse Core Ops, SparseCore 0:
  85.7 192.3 all-reduce.4
  433.8 192.2 all-reduce.6
